TPU v7x, 128 devices: a whole 4x4x4 slice. The times are simulated.
128 devices in a mesh: layer: 8 (over z_hi, x), feat: 16 (over z_lo, y, core).
Axes of the slice: x: 4, y: 4, z: 4 (z_hi: 2, z_lo: 2; z = z_hi * 2 + z_lo), core: 2. Of those that a mesh axis runs over, the one named last changes fastest.
Arguments:
- activations: bfloat16 [4, 1024, 32768], P(None, None, ('layer', 'feat')), may hold values from -6 to 6
- active_blocks: int32 [4, 1024, 256], P(None, None, ('layer', 'feat')), may hold values from 0 to 1, as said below
- cotangent: bfloat16 [4, 1024, 2048], P(None, 'layer', 'feat'), may hold values from -6 to 6
- decoder: bfloat16 [10, 32768, 2048], P(None, ('layer', 'feat')), may hold values from -0.03125 to 0.03125
Outputs:
- decoder_grad: bfloat16 [10, 32768, 2048], P(None, ('layer', 'feat'))
- feature_grad: bfloat16 [4, 1024, 32768], P(None, None, ('layer', 'feat'))
Inputs may be any that keep to these rules, and one draw needn't show every extreme that they name: `active_blocks`: 1 where the block of 128 features is active for that token at that layer, else 0.
All inputs are finite; a program needn't handle non-finite values.
Results may differ from a plain program's by a relative error of at most 0.001.
Values may be sent and summed in bfloat16 or wider, within the bound.
A program may use at most 128 MiB of HBM per device.

v0:
```python
import jax
import jax.numpy as jnp
from jax import lax
from jax.sharding import PartitionSpec as P


def pair_work(sparse, upstream, weights, layers):
    grads = []
    partial_value = jnp.zeros((layers, sparse.shape[1], sparse.shape[2]), jnp.float32)
    offset = 0
    for target in range(layers):
        count = target + 1
        rows = weights[offset : offset + count]
        grads.append(
            jnp.einsum(
                "stf,td->sfd", sparse[:count], upstream[target], preferred_element_type=jnp.float32
            )
        )
        terms = jnp.einsum(
            "td,sfd->stf", upstream[target], rows, preferred_element_type=jnp.float32
        )
        partial_value = partial_value.at[:count].add(terms)
        offset = offset + count
    return (jnp.concatenate(grads, axis=0), partial_value)


def body(activations, active_blocks, cotangent, decoder):
    width = activations.shape[2] // active_blocks.shape[2]
    layers = activations.shape[0]
    feature_mask = jnp.repeat(active_blocks, width, axis=2).astype(jnp.float32)
    sparse = (activations.astype(jnp.float32) * feature_mask).astype(jnp.bfloat16)
    cot_rows = lax.all_gather(cotangent, "layer", axis=1, tiled=True)
    upstream = lax.all_gather(cot_rows, "feat", axis=2, tiled=True)
    weight_grads, partial_value = pair_work(sparse, upstream, decoder, layers)
    feature_grad = (partial_value * feature_mask).astype(jnp.bfloat16)
    return (weight_grads.astype(jnp.bfloat16), feature_grad)


def solution(mesh):
    in_specs = (
        P(None, None, ("layer", "feat")),
        P(None, None, ("layer", "feat")),
        P(None, "layer", "feat"),
        P(None, ("layer", "feat"), None),
    )
    out_specs = (P(None, ("layer", "feat"), None), P(None, None, ("layer", "feat")))
    return jax.shard_map(body, mesh=mesh, in_specs=in_specs, out_specs=out_specs, check_vma=False)
```

profile of v0, /device:TPU:1, one launch (start us, length us, event | category | flops | bytes accessed | tf_op | source)
XLA Modules:
  0.0 217.0 jit_solution(17988041659607771263)
XLA Ops:
  7.2 0.0 all-gather.3.cloned.1.call-start
  7.2 0.7 all-gather.3.cloned.1.call-update
  7.9 0.0 all-gather.5.cloned.1.call-start
  7.9 51.1 %all-gather.3.cloned.1.call-done = bf16[4,1024,128]{2,1,0:T(8,128)(2,1)} async-done(((bf16[4,128,128]{2,1,0:T(8,128)(2,1)}), bf16[4,1024,128]{2,1,0:T(8,128)(2,1)}) %all-gather.3.cloned.1.call-update) | async-done | bytes 1048592 | tf_op jit(solution)/shard_map/all_gather | solution.py:32
  59.1 0.0 all-gather.5.cloned.1.call-update
  59.1 0.8 convert_element_type.18
  59.9 3.0 %copy.6 = bf16[4,1024,256]{1,2,0:T(8,128)(2,1)S(1)} copy(bf16[4,1024,256]{2,1,0:T(8,128)(2,1)} %param.14) | data formatting | bytes 4194304 | tf_op args[0]
  62.9 1.9 fusion
  64.8 94.6 %all-gather.5.cloned.1.call-done = bf16[4,1024,2048]{2,1,0:T(8,128)(2,1)} async-done(((bf16[4,1024,128]{2,1,0:T(8,128)(2,1)}), bf16[4,1024,2048]{2,1,0:T(8,128)(2,1)}) %all-gather.5.cloned.1.call-update) | async-done | bytes 16777232 | tf_op jit(solution)/shard_map/all_gather | solution.py:33
  159.4 3.8 %fusion.15 = f32[1,1024,256]{1,2,0:T(8,128)S(1)} fusion(bf16[4,1024,2048]{2,1,0:T(8,128)(2,1)} %all-gather.5.cloned.1.call-done, bf16[10,256,2048]{2,1,0:T(8,128)(2,1)} %param.17), kind=kOutput, calls=%fused_computation.26 | convolution fusion | flops 1073741824 | bytes 6291456 | tf_op jit(solution)/shard_map/td,sfd->stf/dot_general | solution.py:19
  163.2 0.0 slice-start
  163.2 0.5 scatter-add.10
  163.7 0.0 slice-start.1
  163.7 0.0 slice-start.2
  163.7 5.6 %fusion.14 = f32[4,1024,256]{1,2,0:T(8,128)S(1)} fusion(f32[4,1024,256]{1,2,0:T(8,128)S(1)} %scatter-add.10, bf16[10,256,2048]{2,1,0:T(8,128)(2,1)} %param.17, bf16[4,1024,2048]{2,1,0:T(8,128)(2,1)} %all-gather.5.cloned.1.call-done), kind=kOutput, calls=%fused_computation.25 | convolution fusion | flops 2148007936 | bytes 18874368 | tf_op jit(solution)/shard_map/td,sfd->stf/dot_general | solution.py:19
  169.4 0.0 slice-done
  169.4 0.0 slice-done.1
  169.4 0.0 slice-done.2
  169.4 5.5 %fusion.10 = f32[4,1024,256]{1,2,0:T(8,128)S(1)} fusion(f32[4,1024,256]{1,2,0:T(8,128)S(1)} %fusion.14, bf16[10,256,2048]{2,1,0:T(8,128)(2,1)S(1)} %bitcast.71, bf16[4,1024,2048]{2,1,0:T(8,128)(2,1)} %all-gather.5.cloned.1.call-done), kind=kOutput, calls=%fused_computation.20 | convolution fusion | flops 3222011904 | bytes 20971520 | tf_op jit(solution)/shard_map/td,sfd->stf/dot_general | solution.py:19
  174.9 7.0 %fusion.1 = bf16[4,1024,256]{1,2,0:T(8,128)(2,1)S(1)} fusion(f32[4,1024,256]{1,2,0:T(8,128)S(1)} %fusion.10, f32[4,1024,2]{1,2,0:T(2,128)S(1)} %convert_element_type.18, bf16[10,256,2048]{2,1,0:T(8,128)(2,1)S(1)} %bitcast.71, bf16[4,1024,2048]{2,1,0:T(8,128)(2,1)} %all-gather.5.cloned.1.call-done), kind=kOutput, calls=%fused_computation.4 | convolution fusion | flops 4298113024 | bytes 21004288 | tf_op jit(solution)/shard_map/td,sfd->stf/dot_general | solution.py:19
  181.9 2.6 %copy.7 = bf16[4,1024,256]{2,1,0:T(8,128)(2,1)} copy(bf16[4,1024,256]{1,2,0:T(8,128)(2,1)S(1)} %fusion.1) | data formatting | bytes 4194304
  184.4 0.0 copy-start
  184.4 0.0 slice-start.3
  184.4 0.0 slice-start.4
  184.4 0.0 slice-start.5
  184.4 7.5 %convolution_convert_fusion = bf16[4,256,2048]{2,1,0:T(8,128)(2,1)S(1)} fusion(bf16[4,1024,256]{1,2,0:T(8,128)(2,1)} %fusion, bf16[4,1024,2048]{2,1,0:T(8,128)(2,1)} %all-gather.5.cloned.1.call-done), kind=kOutput, calls=%fused_computation.10 | convolution fusion | flops 4297064448 | bytes 10485760 | tf_op jit(solution)/shard_map/stf,td->sfd/dot_general | solution.py:15
  191.9 0.0 copy-done
  191.9 0.0 slice-start.6
  191.9 6.2 %fusion.9 = bf16[3,256,2048]{2,1,0:T(8,128)(2,1)S(1)} fusion(bf16[4,1024,256]{1,2,0:T(8,128)(2,1)S(1)} %copy-done, bf16[4,1024,2048]{2,1,0:T(8,128)(2,1)} %all-gather.5.cloned.1.call-done), kind=kOutput, calls=%fused_computation.18 | convolution fusion | flops 3222798336 | bytes 9437184 | tf_op jit(solution)/shard_map/stf,td->sfd/dot_general | solution.py:15
  198.1 0.0 slice-done.3
  198.1 0.0 slice-done.4
  198.1 0.0 slice-done.5
  198.1 0.0 slice-done.6
  198.1 2.4 %fusion.11 = bf16[2,256,2048]{2,1,0:T(8,128)(2,1)S(1)} fusion(bf16[4,1024,256]{1,2,0:T(8,128)(2,1)S(1)} %copy-done, bf16[4,1024,2048]{2,1,0:T(8,128)(2,1)S(1)} %bitcast.73), kind=kOutput, calls=%fused_computation.21 | convolution fusion | flops 2148532224 | bytes 8388608 | tf_op jit(solution)/shard_map/stf,td->sfd/dot_general | solution.py:15
  200.5 1.3 fusion.13
  201.8 8.4 %pad_maximum_fusion = bf16[10,256,2048]{2,1,0:T(8,128)(2,1)} fusion(bf16[4,256,2048]{2,1,0:T(8,128)(2,1)S(1)} %convolution_convert_fusion, bf16[3,256,2048]{2,1,0:T(8,128)(2,1)S(1)} %fusion.9, bf16[2,256,2048]{2,1,0:T(8,128)(2,1)S(1)} %fusion.11, bf16[1,256,2048]{2,1,0:T(8,128)(2,1)S(1)} %fusion.13), kind=kLoop, calls=%fused_computation | loop fusion | flops 15728640 | bytes 20971520 | tf_op jit(solution)/shard_map/concatenate | solution.py:24
  (2 shorter events, 0.0 us)
Async XLA Ops:
  7.2 51.9 %all-gather.3.cloned.1.call-start = ((), (), s32[]{:S(2)}) async-start(), calls=%async_computation | async-start | bytes 1179648 | tf_op jit(solution)/shard_map/all_gather | solution.py:32
  7.9 151.5 %all-gather.5.cloned.1.call-start = ((), (), s32[]{:S(2)}) async-start(), calls=%async_computation.1 | async-start | bytes 17825792 | tf_op jit(solution)/shard_map/all_gather | solution.py:33
  163.2 6.2 %slice-start = ((s8[10485760]{0:T(1024)(128)(4,1)}), s8[4194304]{0:T(1024)(128)(4,1)S(1)}, s32[]{:S(2)}) async-start(s8[10485760]{0:T(1024)(128)(4,1)} %bitcast.70), calls=%async_computation.2 | async-start | bytes 8388608
  163.7 5.7 %slice-start.1 = ((s8[10485760]{0:T(1024)(128)(4,1)}), s8[4194304]{0:T(1024)(128)(4,1)S(1)}, s32[]{:S(2)}) async-start(s8[10485760]{0:T(1024)(128)(4,1)} %bitcast.70), calls=%async_computation.3 | async-start | bytes 8388608
  163.7 5.7 %slice-start.2 = ((s8[10485760]{0:T(1024)(128)(4,1)}), s8[2097152]{0:T(1024)(128)(4,1)S(1)}, s32[]{:S(2)}) async-start(s8[10485760]{0:T(1024)(128)(4,1)} %bitcast.70), calls=%async_computation.4 | async-start | bytes 4194304
  184.4 7.5 %copy-start = (bf16[4,1024,256]{1,2,0:T(8,128)(2,1)S(1)}, bf16[4,1024,256]{1,2,0:T(8,128)(2,1)}, u32[]{:S(2)}) copy-start(bf16[4,1024,256]{1,2,0:T(8,128)(2,1)} %fusion) | copy-start | bytes 6291460
  184.4 13.7 %slice-start.3 = ((s8[16777216]{0:T(1024)(128)(4,1)}), s8[4194304]{0:T(1024)(128)(4,1)S(1)}, s32[]{:S(2)}) async-start(s8[16777216]{0:T(1024)(128)(4,1)} %bitcast.72), calls=%async_computation.5 | async-start | bytes 8388608
  184.4 13.7 %slice-start.4 = ((s8[16777216]{0:T(1024)(128)(4,1)}), s8[4194304]{0:T(1024)(128)(4,1)S(1)}, s32[]{:S(2)}) async-start(s8[16777216]{0:T(1024)(128)(4,1)} %bitcast.72), calls=%async_computation.6 | async-start | bytes 8388608
  184.4 13.7 %slice-start.5 = ((s8[16777216]{0:T(1024)(128)(4,1)}), s8[4194304]{0:T(1024)(128)(4,1)S(1)}, s32[]{:S(2)}) async-start(s8[16777216]{0:T(1024)(128)(4,1)} %bitcast.72), calls=%async_computation.7 | async-start | bytes 8388608
  191.9 6.2 %slice-start.6 = ((s8[16777216]{0:T(1024)(128)(4,1)}), s8[4194304]{0:T(1024)(128)(4,1)S(1)}, s32[]{:S(2)}) async-start(s8[16777216]{0:T(1024)(128)(4,1)} %bitcast.72), calls=%async_computation.8 | async-start | bytes 8388608
Sparse Core Ops, SparseCore 0:
  10.3 48.6 all-gather.2
  60.7 98.6 all-gather.4
where the time goes:
time: 217 us
  waiting for transfers between devices  146 us (67%)
  matrix products  39.1 us (18%)
  between operations  14.2 us (7%)
  other arithmetic  11 us (5%)
  local copies, waits for them, and re-layouts  6.11 us (3%)
    all_gather x1, waiting for transfers between devices, body(): upstream = lax.all_gather(cot_rows, 'feat', axis=2, tiled=True)  94.6 us
    all_gather x1, waiting for transfers between devices, body(): cot_rows = lax.all_gather(cotangent, 'layer', axis=1, tiled=True)  51.1 us
    dot_general x4, matrix products, pair_work(): jnp.einsum('td,sfd->stf', upstream[target], rows, preferred_element_type=...  21.9 us
    dot_general x4, matrix products, pair_work(): jnp.einsum('stf,td->sfd', sparse[:count], upstream[target], preferred_ele...  17.3 us
    concatenate x1, other arithmetic, pair_work(): return (jnp.concatenate(grads, axis=0), partial_value)  8.37 us
    unnamed x18, local copies, waits for them, and re-layouts  5.6 us
  transfers between devices with their start and end apart: 2, of which 2 were waited for; matrix products, arithmetic and copies ran while one was open for 3% of the time, Pallas kernels for 0%

commit v1 on v0

v1 whole, which is shorter than its diff:
```python
import functools

import jax
import jax.numpy as jnp
from jax import lax
from jax.experimental import pallas as pl
from jax.experimental.pallas import tpu as pltpu
from jax.sharding import PartitionSpec as P

MESH = pl.DeviceIdType.MESH
LAYERS, TOKENS, D, WIDTH = 4, 1024, 2048, 256
PAIRS = LAYERS * (LAYERS + 1) // 2
ROWS = {3: (48, 48, 32), 2: (48, 32, 48), 1: (32, 48, 48), 0: (48, 48, 32)}
START = {g: (0, r[0], r[0] + r[1]) for g, r in ROWS.items()}
ORDER = ((0, 1, 2), (1, 2, 0), (2, 0, 1))
TARGETS = (3, 2, 1, 0)
OFFSET = (0, 1, 3, 6)
BUFS = [(g, a) for g in range(LAYERS) for a in range(3)]
BF16, F32 = jnp.bfloat16, jnp.float32


def position():
    layer, feat = lax.axis_index("layer"), lax.axis_index("feat")
    x, zh = lax.rem(layer, 4), layer // 4
    core, y, zl = lax.rem(feat, 2), lax.rem(feat // 2, 4), feat // 8
    return (x, y, zh * 2 + zl), core


def device_id(c, core):
    x, y, z = c
    return ((z // 2) * 4 + x, (lax.rem(z, 2) * 4 + y) * 2 + core)


def shifted(c, axis, by):
    return tuple(lax.rem(v + by + 4, 4) if i == axis else v for i, v in enumerate(c))


class Gather:
    def __init__(self, own_ref, bufs, own_sem, send, recv):
        self.c, self.core = position()
        self.own_ref, self.bufs = own_ref, dict(zip(BUFS, bufs))
        self.own_sem, self.send, self.recv = own_sem, send, recv
        self.sends, self.copies = [], {}

    def near(self, axis, by):
        return device_id(shifted(self.c, axis, by), self.core)

    def barrier(self):
        sem = pltpu.get_barrier_semaphore()
        peers = [self.near(axis, by) for axis in range(3) for by in (1, -1)]
        peers.append(device_id(self.c, 1 - self.core))
        for peer in peers:
            pl.semaphore_signal(sem, inc=1, device_id=peer, device_id_type=MESH)
        pl.semaphore_wait(sem, len(peers))

    def own(self):
        out = []
        for i, (g, a) in enumerate(BUFS):
            c1, c2, c3 = (self.c[k] for k in ORDER[a])
            out.append(pltpu.make_async_copy(
                self.own_ref.at[g, pl.ds(START[g][a], ROWS[g][a])],
                self.bufs[g, a].at[self.core, c3, c2, c1], self.own_sem.at[i]))
        return out

    def view(self, g, a, key, c):
        c1, c2, c3 = (c[k] for k in ORDER[a])
        buf = self.bufs[g, a].at[self.core]
        if key[0] == "1":
            return buf.at[c3, c2, c1]
        if key[0] == "2":
            return buf.at[c3, c2]
        if key[0] == "3":
            return buf.at[c3, pl.ds(2 * int(key[1]), 2)]
        return buf.at[c3]

    SLOTS = ("1L", "1R", "1O", "2L", "2R", "2O", "30L", "31L", "30R", "31R", "30O", "31O",
             "p0", "pL", "pR", "pO")

    def copy(self, g, a, slot, src, to):
        i = (g * 3 + a) * len(self.SLOTS) + self.SLOTS.index(slot)
        return pltpu.make_async_remote_copy(
            src_ref=src, dst_ref=src, send_sem=self.send.at[i], recv_sem=self.recv.at[i],
            device_id=to, device_id_type=MESH)

    def start(self, g, a, slot, key, by):
        phase = slot[0]
        if phase == "p":
            src = self.view(g, a, "p", shifted(self.c, ORDER[a][2], by))
            to = device_id(self.c, 1 - self.core)
        else:
            axis = ORDER[a][int(phase) - 1]
            src = self.view(g, a, key, shifted(self.c, axis, by))
            if slot[-1] == "O":
                step = -by
            else:
                step = 1 if slot[-1] == "L" else -1
            to = self.near(axis, step)
        copy = self.copy(g, a, slot, src, to)
        copy.start()
        self.copies[g, a, slot] = copy

    def wait(self, g, a, slot):
        self.copies[g, a, slot].wait_recv()

    def p1_start(self, g):
        for a in range(3):
            self.start(g, a, "1L", "1", 0)
            self.start(g, a, "1R", "1", 0)

    def p1_forward(self, g):
        for a in range(3):
            self.wait(g, a, "1L")
            self.wait(g, a, "1R")
            self.start(g, a, "1O", "1", -1 if (g + a) % 2 else 1)

    def p2_start(self, g):
        for a in range(3):
            self.wait(g, a, "1O")
            self.start(g, a, "2L", "2", 0)
            self.start(g, a, "2R", "2", 0)

    def p2_forward(self, g):
        for a in range(3):
            self.wait(g, a, "2L")
            self.wait(g, a, "2R")
            self.start(g, a, "2O", "2", -1 if (g + a) % 2 else 1)

    def p3_start(self, g):
        for a in range(3):
            self.wait(g, a, "2O")
            self.start(g, a, "30L", "30", 0)
            self.start(g, a, "31R", "31", 0)
            self.start(g, a, "31L", "31", 0)
            self.start(g, a, "30R", "30", 0)
            self.start(g, a, "p0", "p", 0)

    def p3_forward(self, g):
        for a in range(3):
            self.wait(g, a, "30L")
            self.start(g, a, "30O", "30", -1)
            self.wait(g, a, "31R")
            self.start(g, a, "31O", "31", 1)

    def partner_sides(self, g):
        for a in range(3):
            self.wait(g, a, "31L")
            self.start(g, a, "pL", "p", -1)
            self.wait(g, a, "30R")
            self.start(g, a, "pR", "p", 1)

    def partner_last(self, g):
        for a in range(3):
            self.wait(g, a, "30O")
            self.wait(g, a, "31O")
            self.start(g, a, "pO", "p", 2)

    def arrived(self, g):
        for a in range(3):
            for slot in ("p0", "pL", "pR", "pO"):
                self.wait(g, a, slot)

    def finish(self):
        for copy in self.copies.values():
            copy.wait_send()


def gather_kernel(own_ref, *rest):
    bufs, (own_sem, send, recv) = rest[:12], rest[12:]
    net = Gather(own_ref, bufs, own_sem, send, recv)
    own = net.own()
    for copy in own:
        copy.start()
    net.barrier()
    for copy in own:
        copy.wait()
    for g in TARGETS:
        net.p1_start(g)
    for g in TARGETS:
        net.p1_forward(g)
    net.p2_start(3)
    net.p2_start(2)
    net.p2_forward(3)
    net.p2_forward(2)
    net.p3_start(3)
    net.p2_start(1)
    net.p3_forward(3)
    net.p2_forward(1)
    net.p3_start(2)
    net.p2_start(0)
    net.partner_sides(3)
    net.p3_forward(2)
    net.partner_last(3)
    net.p2_forward(0)
    net.p3_start(1)
    net.partner_sides(2)
    net.p3_forward(1)
    net.partner_last(2)
    net.arrived(3)
    net.p3_start(0)
    net.partner_sides(1)
    net.p3_forward(0)
    net.partner_last(1)
    net.arrived(2)
    net.partner_sides(0)
    net.partner_last(0)
    net.arrived(1)
    net.arrived(0)
    net.finish()


def gather(cotangent):
    sems = len(BUFS) * len(Gather.SLOTS)
    return pl.pallas_call(
        gather_kernel,
        out_shape=[pltpu.VMEM((2, 4, 4, 4, ROWS[g][a], 128), BF16) for g, a in BUFS],
        in_specs=[pl.BlockSpec(memory_space=pl.ANY)],
        out_specs=[pl.BlockSpec(memory_space=pltpu.VMEM)] * len(BUFS),
        scratch_shapes=[
            pltpu.SemaphoreType.DMA((len(BUFS),)),
            pltpu.SemaphoreType.DMA((sems,)),
            pltpu.SemaphoreType.DMA((sems,)),
        ],
        compiler_params=pltpu.CompilerParams(collective_id=0, has_side_effects=True, vmem_limit_bytes=2 * 2**20),
        name="torus_gather",
    )(cotangent)


def block(bufs, g, x, y, z, core):
    parts = []
    for a in range(3):
        c1, c2, c3 = ((x, y, z)[k] for k in ORDER[a])
        parts.append(bufs[g, a][core, c3, c2, c1])
    return jnp.concatenate(parts, axis=0)


def columns(bufs, g, q):
    zl, y = q // 4, lax.rem(q, 4)
    return jnp.concatenate(
        [jnp.concatenate([block(bufs, g, l % 4, y, (l // 4) * 2 + zl, core) for l in range(8)], axis=0)
         for core in range(2)], axis=1)


def rows(bufs, g, h):
    zh = h // 2
    out = []
    for i in range(2):
        x = lax.rem(h, 2) * 2 + i
        out.append(jnp.concatenate(
            [block(bufs, g, x, (f // 2) % 4, zh * 2 + f // 8, f % 2) for f in range(16)], axis=1))
    return jnp.concatenate(out, axis=0)


def prepare(act, mask, sparse_t, mask_cols):
    for s in range(LAYERS):
        @pl.loop(0, 8)
        def _(l):
            tok = pl.ds(pl.multiple_of(l * 128, 128), 128)
            for b in range(2):
                m = jnp.broadcast_to(mask[s, b:b + 1, tok].astype(F32), (128, 128))
                values = act[s, tok, b * 128:(b + 1) * 128].astype(F32).T
                sparse_t[s, b * 128:(b + 1) * 128, tok] = (values * m).astype(BF16)
                mask_cols[s, tok, b * 128:(b + 1) * 128] = m.T.astype(BF16)


def grad_step(bufs, g, q, sparse_t, store):
    lhs = sparse_t[0:g + 1].reshape((g + 1) * WIDTH, TOKENS)
    out = jnp.dot(lhs, columns(bufs, g, q), preferred_element_type=F32).astype(BF16)
    store(q, out.reshape(g + 1, WIDTH, 256))


def feature_step(bufs, g, h, dec, total, first):
    tok = pl.ds(pl.multiple_of(h * 256, 256), 256)
    lhs = rows(bufs, g, h)
    for s in range(g + 1):
        term = lax.dot_general(lhs, dec[s], (((1,), (1,)), ((), ())), preferred_element_type=F32)
        if first:
            total[s, tok] = term
        else:
            total[s, tok] += term


def compute_kernel(act_hbm, mask, dec_hbm, *rest):
    bufs = dict(zip(BUFS, rest[:12]))
    grad_hbm, feat_hbm, act, sparse_t, mask_cols, dec, total, grad, feat, sem = rest[12:]
    loads = [pltpu.make_async_copy(act_hbm, act, sem.at[0])]
    for g in TARGETS:
        loads.append(pltpu.make_async_copy(dec_hbm.at[pl.ds(OFFSET[g], g + 1)], dec.at[pl.ds(OFFSET[g], g + 1)], sem.at[1 + g]))
    for load in loads:
        load.start()
    loads[0].wait()
    prepare(act, mask, sparse_t, mask_cols)
    stores = []
    for i, g in enumerate(TARGETS):
        base = OFFSET[g]
        def store(q, out):
            grad[base:base + g + 1, :, pl.ds(pl.multiple_of(q * 256, 256), 256)] = out
        @pl.loop(0, 8)
        def _(q):
            grad_step(bufs, g, q, sparse_t, store)
        out = pltpu.make_async_copy(grad.at[pl.ds(base, g + 1)], grad_hbm.at[pl.ds(base, g + 1)], sem.at[5 + g])
        out.start()
        stores.append(out)
        loads[1 + i].wait()
        @pl.loop(0, 4)
        def _(h):
            feature_step(bufs, g, h, dec.at[pl.ds(base, g + 1)], total, i == 0)
    for s in range(LAYERS):
        @pl.loop(0, 8)
        def _(l):
            tok = pl.ds(pl.multiple_of(l * 128, 128), 128)
            feat[s, tok] = (total[s, tok] * mask_cols[s, tok].astype(F32)).astype(BF16)
        out = pltpu.make_async_copy(feat.at[s], feat_hbm.at[s], sem.at[9 + s])
        out.start()
        stores.append(out)
    for out in stores:
        out.wait()


def compute(act, mask, dec, bufs):
    vmem = pl.BlockSpec(memory_space=pltpu.VMEM)
    hbm = pl.BlockSpec(memory_space=pl.ANY)
    return pl.pallas_call(
        compute_kernel,
        out_shape=[jax.ShapeDtypeStruct((PAIRS, WIDTH, D), BF16), jax.ShapeDtypeStruct((LAYERS, TOKENS, WIDTH), BF16)],
        in_specs=[hbm, vmem, hbm] + [vmem] * len(BUFS),
        out_specs=[hbm, hbm],
        scratch_shapes=[
            pltpu.VMEM((LAYERS, TOKENS, WIDTH), BF16),
            pltpu.VMEM((LAYERS, WIDTH, TOKENS), BF16),
            pltpu.VMEM((LAYERS, TOKENS, WIDTH), BF16),
            pltpu.VMEM((PAIRS, WIDTH, D), BF16),
            pltpu.VMEM((LAYERS, TOKENS, WIDTH), F32),
            pltpu.VMEM((PAIRS, WIDTH, D), BF16),
            pltpu.VMEM((LAYERS, TOKENS, WIDTH), BF16),
            pltpu.SemaphoreType.DMA((16,)),
        ],
        compiler_params=pltpu.CompilerParams(vmem_limit_bytes=44 * 2**20),
        name="pair_products",
    )(act, mask, dec, *bufs)


def body(activations, active_blocks, cotangent, decoder):
    bufs = gather(cotangent)
    mask = jnp.transpose(active_blocks, (0, 2, 1))
    return tuple(compute(activations, mask, decoder, bufs))


def solution(mesh):
    in_specs = (
        P(None, None, ("layer", "feat")),
        P(None, None, ("layer", "feat")),
        P(None, "layer", "feat"),
        P(None, ("layer", "feat"), None),
    )
    out_specs = (P(None, ("layer", "feat"), None), P(None, None, ("layer", "feat")))
    return jax.shard_map(body, mesh=mesh, in_specs=in_specs, out_specs=out_specs, check_vma=False)
```

time: 217 us -> 106 us (0.49)
  waiting for transfers between devices: 146 us -> 0 us
  Pallas kernels: 0 us -> 98 us
  matrix products: 39.1 us -> 0 us
  between operations: 14.2 us -> 0.66 us
  other arithmetic: 11 us -> 0 us
    all_gather x2 -> x0, waiting for transfers between devices: 146 us -> none  [the longest x1 94.6 us: body(): upstream = lax.all_gather(cot_rows, 'feat', axis=2, tiled=True)]
    pallas_call x0 -> x2, Pallas kernels: none -> 98 us  [the longest x1 57.5 us: gather(): pl.pallas_call(gather_kernel, out_shape=[pltpu.VMEM((2, 4, 4, 4, ROWS[g][...]
    dot_general x8 -> x0, matrix products: 39.1 us -> none  [the longest x4 21.9 us: pair_work(): jnp.einsum('td,sfd->stf', upstream[target], rows, preferred_element_type=...]
    concatenate x1 -> x0, other arithmetic: 8.37 us -> none  [pair_work(): return (jnp.concatenate(grads, axis=0), partial_value)]
    convert_element_type x2 -> x0, other arithmetic: 2.67 us -> none  [the longest x1 1.9 us: body(): (activations.astype(jnp.float32) * feature_mask).astype(jnp.bfloat16)]
    unnamed x18 -> x14, local copies, waits for them, and re-layouts: 5.6 us -> 7.41 us
  transfers between devices with their start and end apart: 2 -> 0, of which waited for: 2 -> 0; matrix products, arithmetic and copies ran while one was open for 3% -> 0% of each run, Pallas kernels for 0% -> 0%
where the time goes in v1:
time: 106 us
  Pallas kernels  98 us (92%)
  local copies, waits for them, and re-layouts  7.41 us (7%)
    pallas_call x1, Pallas kernels, gather(): pl.pallas_call(gather_kernel, out_shape=[pltpu.VMEM((2, 4, 4, 4, ROWS[g][...  57.5 us
    pallas_call x1, Pallas kernels, compute(): pl.pallas_call(compute_kernel, out_shape=[jax.ShapeDtypeStruct((PAIRS, WI...  40.5 us
    unnamed x14, local copies, waits for them, and re-layouts  7.41 us

profile of v1, /device:TPU:1, one launch (start us, length us, event | category | flops | bytes accessed | tf_op | source)
XLA Modules:
  0.0 106.1 jit_solution(12604960399776390786)
XLA Ops:
  0.6 0.0 copy-start.5
  0.6 0.9 copy-done.5
  1.5 57.5 %torus_gather.1 = (bf16[2,4,4,4,48,128]{5,4,3,2,1,0:T(8,128)(2,1)S(1)}, bf16[2,4,4,4,48,128]{5,4,3,2,1,0:T(8,128)(2,1)S(1)}, bf16[2,4,4,4,32,128]{5,4,3,2,1,0:T(...) custom-call(bf16[4,128,128]{2,1,0:T(8,128)(2,1)S(1)} %copy-done.5), custom_call_target="tpu_custom_call" | custom-call | tf_op jit(solution)/shard_map/torus_gather/pallas_call | solution.py:213
  59.0 0.0 copy-start
  59.0 1.1 %copy-done = bf16[2,4,4,4,48,128]{5,4,3,2,1,0:T(8,128)(2,1)} copy-done((bf16[2,4,4,4,48,128]{5,4,3,2,1,0:T(8,128)(2,1)}, bf16[2,4,4,4,48,128]{5,4,3,2,1,0:T(8,128)(2,1)S(1)}, u32[]{:S(2)}) %copy-start) | copy-done | bytes 1572888
  60.2 0.0 copy-start.1
  60.2 1.2 %copy-done.1 = bf16[2,4,4,4,48,128]{5,4,3,2,1,0:T(8,128)(2,1)} copy-done((bf16[2,4,4,4,48,128]{5,4,3,2,1,0:T(8,128)(2,1)}, bf16[2,4,4,4,48,128]{5,4,3,2,1,0:T(8,128)(2,1)S(1)}, u32[]{:S(2)}) %copy-start.1) | copy-done | bytes 1572888
  61.3 0.0 copy-start.2
  61.3 1.1 %copy-done.2 = bf16[2,4,4,4,48,128]{5,4,3,2,1,0:T(8,128)(2,1)} copy-done((bf16[2,4,4,4,48,128]{5,4,3,2,1,0:T(8,128)(2,1)}, bf16[2,4,4,4,48,128]{5,4,3,2,1,0:T(8,128)(2,1)S(1)}, u32[]{:S(2)}) %copy-start.2) | copy-done | bytes 1572888
  62.5 0.0 copy-start.3
  62.5 1.2 %copy-done.3 = bf16[2,4,4,4,48,128]{5,4,3,2,1,0:T(8,128)(2,1)} copy-done((bf16[2,4,4,4,48,128]{5,4,3,2,1,0:T(8,128)(2,1)}, bf16[2,4,4,4,48,128]{5,4,3,2,1,0:T(8,128)(2,1)S(1)}, u32[]{:S(2)}) %copy-start.3) | copy-done | bytes 1572888
  63.7 0.0 copy-start.4
  63.7 1.1 %copy-done.4 = bf16[2,4,4,4,48,128]{5,4,3,2,1,0:T(8,128)(2,1)} copy-done((bf16[2,4,4,4,48,128]{5,4,3,2,1,0:T(8,128)(2,1)}, bf16[2,4,4,4,48,128]{5,4,3,2,1,0:T(8,128)(2,1)S(1)}, u32[]{:S(2)}) %copy-start.4) | copy-done | bytes 1572888
  64.8 0.0 copy-start.6
  64.8 0.8 copy-done.6
  65.6 40.5 %pair_products.1 = (bf16[10,256,2048]{2,1,0:T(8,128)(2,1)}, bf16[4,1024,256]{2,1,0:T(8,128)(2,1)}) custom-call(bf16[4,1024,256]{2,1,0:T(8,128)(2,1)} %act_hbm.1, s32[4,2,1024]{2,1,0:T(2,128)S(1)} %bitcast.1, bf16[10,256,2048]{2,1,0:T(8,128)(2,1)} %dec_hbm.1, bf16[2,4,4,4,48,128]{5,4,3,2,1,0:T(8,128)(2,1)S(1)} %get-tuple-element.14.rest_0_, ...), custom_call_target="tpu_custom_call" | custom-call | tf_op jit(solution)/shard_map/pair_products/pallas_call | solution.py:322
Async XLA Ops:
  0.6 0.9 copy-start.5
  59.0 1.1 %copy-start = (bf16[2,4,4,4,48,128]{5,4,3,2,1,0:T(8,128)(2,1)}, bf16[2,4,4,4,48,128]{5,4,3,2,1,0:T(8,128)(2,1)S(1)}, u32[]{:S(2)}) copy-start(bf16[2,4,4,4,48,128]{5,4,3,2,1,0:T(8,128)(2,1)S(1)} %get-tuple-element.19.rest_5_) | copy-start | bytes 4718596
  60.2 1.2 %copy-start.1 = (bf16[2,4,4,4,48,128]{5,4,3,2,1,0:T(8,128)(2,1)}, bf16[2,4,4,4,48,128]{5,4,3,2,1,0:T(8,128)(2,1)S(1)}, u32[]{:S(2)}) copy-start(bf16[2,4,4,4,48,128]{5,4,3,2,1,0:T(8,128)(2,1)S(1)} %get-tuple-element.20.rest_6_) | copy-start | bytes 4718596
  61.3 1.1 %copy-start.2 = (bf16[2,4,4,4,48,128]{5,4,3,2,1,0:T(8,128)(2,1)}, bf16[2,4,4,4,48,128]{5,4,3,2,1,0:T(8,128)(2,1)S(1)}, u32[]{:S(2)}) copy-start(bf16[2,4,4,4,48,128]{5,4,3,2,1,0:T(8,128)(2,1)S(1)} %get-tuple-element.22.rest_8_) | copy-start | bytes 4718596
  62.5 1.2 %copy-start.3 = (bf16[2,4,4,4,48,128]{5,4,3,2,1,0:T(8,128)(2,1)}, bf16[2,4,4,4,48,128]{5,4,3,2,1,0:T(8,128)(2,1)S(1)}, u32[]{:S(2)}) copy-start(bf16[2,4,4,4,48,128]{5,4,3,2,1,0:T(8,128)(2,1)S(1)} %get-tuple-element.23.rest_9_) | copy-start | bytes 4718596
  63.7 1.1 %copy-start.4 = (bf16[2,4,4,4,48,128]{5,4,3,2,1,0:T(8,128)(2,1)}, bf16[2,4,4,4,48,128]{5,4,3,2,1,0:T(8,128)(2,1)S(1)}, u32[]{:S(2)}) copy-start(bf16[2,4,4,4,48,128]{5,4,3,2,1,0:T(8,128)(2,1)S(1)} %get-tuple-element.24.rest_10_) | copy-start | bytes 4718596
  64.8 0.8 copy-start.6

commit v2 on v0

v2 whole, which is shorter than its diff:
```python
import functools

import jax
import jax.numpy as jnp
from jax import lax
from jax.experimental import pallas as pl
from jax.experimental.pallas import tpu as pltpu
from jax.sharding import PartitionSpec as P

MESH = pl.DeviceIdType.MESH
LAYERS, TOKENS, D, WIDTH = 4, 1024, 2048, 256
PAIRS = LAYERS * (LAYERS + 1) // 2
ROWS = {3: (48, 48, 32), 2: (48, 32, 48), 1: (32, 48, 48), 0: (48, 48, 32)}
START = {g: (0, r[0], r[0] + r[1]) for g, r in ROWS.items()}
ORDER = ((0, 1, 2), (1, 2, 0), (2, 0, 1))
TARGETS = (3, 2, 1, 0)
OFFSET = (0, 1, 3, 6)
BUFS = [(g, a) for g in range(LAYERS) for a in range(3)]
BF16, F32 = jnp.bfloat16, jnp.float32
DIRECT = (3,)
EARLY_LIMIT, LATE_LIMIT = 32 * 2**20, 6 * 2**20


def position():
    layer, feat = lax.axis_index("layer"), lax.axis_index("feat")
    x, zh = lax.rem(layer, 4), layer // 4
    core, y, zl = lax.rem(feat, 2), lax.rem(feat // 2, 4), feat // 8
    return (x, y, zh * 2 + zl), core


def device_id(c, core):
    x, y, z = c
    return ((z // 2) * 4 + x, (lax.rem(z, 2) * 4 + y) * 2 + core)


def shifted(c, axis, by):
    return tuple(lax.rem(v + by + 4, 4) if i == axis else v for i, v in enumerate(c))


class Gather:
    SLOTS = ("1L", "1R", "1O", "2L", "2R", "2O", "3L0", "3L1", "3R0", "3R1", "3O0", "3O1", "p0", "pL", "pR", "pO")

    def __init__(self, own_ref, bufs, own_sem, send, recv):
        self.c, self.core = position()
        self.own_ref, self.bufs = own_ref, bufs
        self.own_sem, self.send, self.recv = own_sem, send, recv

    def near(self, axis, by):
        return device_id(shifted(self.c, axis, by), self.core)

    def greet(self):
        sem = pltpu.get_barrier_semaphore()
        for peer in self.peers():
            pl.semaphore_signal(sem, inc=1, device_id=peer, device_id_type=MESH)

    def peers(self):
        out = [self.near(axis, by) for axis in range(3) for by in (1, -1, 2)]
        return out + [device_id(self.c, 1 - self.core)]

    def meet(self):
        pl.semaphore_wait(pltpu.get_barrier_semaphore(), 10)

    def own(self):
        out = []
        for i, (g, a) in enumerate(BUFS):
            c1, c2, c3 = (self.c[k] for k in ORDER[a])
            out.append(pltpu.make_async_copy(
                self.own_ref.at[g, pl.ds(START[g][a], ROWS[g][a])],
                self.bufs[g, a].at[self.core, c3, c2, c1], self.own_sem.at[i]))
        return out

    def copy(self, g, a, slot):
        phase, side = slot[0], slot[1]
        axis = ORDER[a][2 if phase == "p" else int(phase) - 1]
        by = 0
        if phase == "p":
            by = {"0": 0, "L": -1, "R": 1, "O": 2}[side]
            to = device_id(self.c, 1 - self.core)
        elif side == "O":
            if phase == "1" or (phase == "2" and g in DIRECT):
                to = self.near(axis, 2)
            else:
                by = (-1 if slot[2] == "0" else 1) if phase == "3" else (-1 if (g + a) % 2 else 1)
                to = self.near(axis, -by)
        else:
            to = self.near(axis, 1 if side == "L" else -1)
        c1, c2, c3 = (shifted(self.c, axis, by)[k] for k in ORDER[a])
        buf = self.bufs[g, a].at[self.core, c3]
        if phase == "1":
            buf = buf.at[c2, c1]
        elif phase == "2":
            buf = buf.at[c2]
        elif phase == "3":
            buf = buf.at[pl.ds(2 * int(slot[2]), 2)]
        i = (g * 3 + a) * len(self.SLOTS) + self.SLOTS.index(slot)
        return pltpu.make_async_remote_copy(
            src_ref=buf, dst_ref=buf, send_sem=self.send.at[i], recv_sem=self.recv.at[i],
            device_id=to, device_id_type=MESH)

    def go(self, g, a, *slots):
        for slot in slots:
            self.copy(g, a, slot).start()

    def wait(self, g, a, *slots):
        for slot in slots:
            self.copy(g, a, slot).wait_recv()

    def p1(self, g):
        for a in range(3):
            self.go(g, a, "1O", "1L", "1R")

    def p2(self, g):
        for a in range(3):
            self.wait(g, a, "1O", "1L", "1R")
            if g in DIRECT:
                self.go(g, a, "2O")
            self.go(g, a, "2L", "2R")

    def p2_forward(self, g):
        for a in range(3):
            self.wait(g, a, "2L", "2R")
            self.go(g, a, "2O")

    def p3(self, g):
        for a in range(3):
            if g in DIRECT:
                self.wait(g, a, "2L", "2R")
            self.wait(g, a, "2O")
            self.go(g, a, "3L0", "3R1", "3L1", "3R0")
        for a in range(3):
            self.go(g, a, "p0")

    def p3_forward(self, g):
        for a in range(3):
            self.wait(g, a, "3L0")
            self.go(g, a, "3O0")
            self.wait(g, a, "3R1")
            self.go(g, a, "3O1")

    def sides(self, g):
        for a in range(3):
            self.wait(g, a, "3L1")
            self.go(g, a, "pL")
            self.wait(g, a, "3R0")
            self.go(g, a, "pR")

    def last(self, g):
        for a in range(3):
            self.wait(g, a, "3O0", "3O1")
            self.go(g, a, "pO")

    def arrived(self, g):
        for a in range(3):
            self.wait(g, a, "p0", "pL", "pR", "pO")

    def finish(self):
        for g, a in BUFS:
            for slot in self.SLOTS:
                self.copy(g, a, slot).wait_send()


def block(bufs, g, x, y, z, core):
    parts = []
    for a in range(3):
        c1, c2, c3 = ((x, y, z)[k] for k in ORDER[a])
        parts.append(bufs[g, a][core, c3, c2, c1])
    return jnp.concatenate(parts, axis=0)


def columns(bufs, g, q):
    zl, y = q // 4, lax.rem(q, 4)
    return jnp.concatenate(
        [jnp.concatenate([block(bufs, g, l % 4, y, (l // 4) * 2 + zl, core) for l in range(8)], axis=0)
         for core in range(2)], axis=1)


def rows(bufs, g, h):
    zh = h // 2
    out = []
    for i in range(2):
        x = lax.rem(h, 2) * 2 + i
        out.append(jnp.concatenate(
            [block(bufs, g, x, (f // 2) % 4, zh * 2 + f // 8, f % 2) for f in range(16)], axis=1))
    return jnp.concatenate(out, axis=0)


def prepare(s, act, mask, sparse_t, mask_cols):
    @pl.loop(0, 8)
    def _(l):
        tok = pl.ds(pl.multiple_of(l * 128, 128), 128)
        for b in range(2):
            m = jnp.broadcast_to(mask[s, b:b + 1, tok].astype(F32), (128, 128))
            values = act[s, tok, b * 128:(b + 1) * 128].astype(F32).T
            sparse_t[s, b * 128:(b + 1) * 128, tok] = (values * m).astype(BF16)
            mask_cols[s, tok, b * 128:(b + 1) * 128] = m.T.astype(BF16)


def grad_step(bufs, g, q, sparse_t, grad, base):
    lhs = sparse_t[0:g + 1].reshape((g + 1) * WIDTH, TOKENS)
    out = jnp.dot(lhs, columns(bufs, g, q), preferred_element_type=F32).astype(BF16)
    grad[base:base + g + 1, :, pl.ds(pl.multiple_of(q * 256, 256), 256)] = out.reshape(g + 1, WIDTH, 256)


def feature_step(bufs, g, h, dec, base, total, finish):
    tok = pl.ds(pl.multiple_of(h * 256, 256), 256)
    lhs = rows(bufs, g, h)
    for s in range(g + 1):
        term = lax.dot_general(lhs, dec[base + s], (((1,), (1,)), ((), ())), preferred_element_type=F32)
        if g < LAYERS - 1:
            term = term + total[s, tok]
        if s == g:
            finish(s, tok, term)
        else:
            total[s, tok] = term


def at(table, i):
    for when, events in table:
        @pl.when(i == when)
        def _():
            for event in events:
                event()


def early_kernel(own_ref, act_hbm, mask_hbm, dec_hbm, *rest):
    buf0, (grad, feat, total0, sparse_t, mask_cols, dec0) = rest[:3], rest[3:9]
    later, (act, mask, dec, total, own_sem, send, recv, sem) = rest[9:18], rest[18:]
    bufs = {(g, a): buf0[a] if g == 0 else later[(g - 1) * 3 + a] for g, a in BUFS}
    net = Gather(own_ref, bufs, own_sem, send, recv)
    own = net.own()
    for copy in own:
        copy.start()
    load_act = pltpu.make_async_copy(act_hbm, act, sem.at[0])
    load_mask = pltpu.make_async_copy(mask_hbm, mask, sem.at[5])
    load_act.start()
    load_mask.start()
    net.greet()
    for copy in own:
        copy.wait()
    net.meet()
    for g in TARGETS:
        net.p1(g)
    loads = [pltpu.make_async_copy(dec_hbm.at[pl.ds(6, 4)], dec.at[pl.ds(5, 4)], sem.at[1]),
             pltpu.make_async_copy(dec_hbm.at[pl.ds(3, 3)], dec.at[pl.ds(2, 3)], sem.at[2]),
             pltpu.make_async_copy(dec_hbm.at[pl.ds(1, 2)], dec.at[pl.ds(0, 2)], sem.at[3]),
             pltpu.make_async_copy(dec_hbm.at[pl.ds(0, 1)], dec0, sem.at[4])]
    for load in loads:
        load.start()
    load_act.wait()
    load_mask.wait()
    prepare(0, act, mask, sparse_t, mask_cols)
    prepare(1, act, mask, sparse_t, mask_cols)
    net.p2(3)
    net.p2(2)
    prepare(2, act, mask, sparse_t, mask_cols)
    prepare(3, act, mask, sparse_t, mask_cols)
    net.p3(3)
    net.p2(1)
    net.p2_forward(2)
    net.p3_forward(3)
    net.p2_forward(1)
    net.sides(3)
    net.p3(2)
    net.p2(0)
    net.last(3)
    net.arrived(3)

    def finish(s, tok, term):
        feat[s - 1, tok] = (term * mask_cols[s, tok].astype(F32)).astype(BF16)

    plan = {
        3: ([(1, [lambda: net.p3_forward(2)]), (2, [lambda: net.p2_forward(0), lambda: net.p3(1)]), (5, [lambda: net.sides(2)])],
            [(0, [lambda: net.last(2)]), (3, [lambda: net.p3_forward(1), lambda: net.p3(0)])]),
        2: ([(2, [lambda: net.sides(1)]), (6, [lambda: net.last(1)])],
            [(1, [lambda: net.p3_forward(0)])]),
        1: ([(1, [lambda: net.sides(0)]), (6, [lambda: net.last(0)])], []),
    }
    for i, g in enumerate((3, 2, 1)):
        base = OFFSET[g] - 1
        if g < 3:
            net.arrived(g)
        loads[i].wait()

        @pl.loop(0, 8)
        def _(q):
            at(plan[g][0], q)
            grad_step(bufs, g, q, sparse_t, grad, base)

        @pl.loop(0, 4)
        def _(h):
            at(plan[g][1], h)
            feature_step(bufs, g, h, dec, base, TOTAL(total, total0), finish)
    loads[3].wait()
    net.arrived(0)
    net.finish()


class TOTAL:
    def __init__(self, rest, first):
        self.rest, self.first = rest, first

    def __getitem__(self, key):
        s, tok = key
        return self.first[tok] if s == 0 else self.rest[s - 1, tok]

    def __setitem__(self, key, value):
        s, tok = key
        if s == 0:
            self.first[tok] = value
        else:
            self.rest[s - 1, tok] = value


def late_kernel(*refs):
    buf0, (grad_in, feat_in, total0, sparse_t, mask_cols, dec0), (grad_hbm, feat_hbm, grad, feat, sem) = refs[:3], refs[3:9], refs[9:]
    bufs = {(0, a): buf0[a] for a in range(3)}
    stores = [pltpu.make_async_copy(grad_in, grad_hbm.at[pl.ds(1, PAIRS - 1)], sem.at[0]),
              pltpu.make_async_copy(feat_in, feat_hbm.at[pl.ds(1, LAYERS - 1)], sem.at[1])]
    for out in stores:
        out.start()

    def finish(s, tok, term):
        feat[tok] = (term * mask_cols[0, tok].astype(F32)).astype(BF16)

    @pl.loop(0, 4)
    def _(h):
        feature_step(bufs, 0, h, dec0.at[pl.ds(0, 1)], 0, TOTAL(None, total0), finish)
    stores.append(pltpu.make_async_copy(feat, feat_hbm.at[0], sem.at[2]))
    stores[-1].start()

    @pl.loop(0, 8)
    def _(q):
        grad_step(bufs, 0, q, sparse_t, grad, 0)
    stores.append(pltpu.make_async_copy(grad, grad_hbm.at[pl.ds(0, 1)], sem.at[3]))
    stores[-1].start()
    for out in stores:
        out.wait()


def body(activations, active_blocks, cotangent, decoder):
    vmem, hbm = pl.BlockSpec(memory_space=pltpu.VMEM), pl.BlockSpec(memory_space=pltpu.HBM)
    mask = pltpu.with_memory_space_constraint(jnp.transpose(active_blocks, (0, 2, 1)), pltpu.HBM)
    cotangent = pltpu.with_memory_space_constraint(cotangent, pltpu.HBM)
    sems = len(BUFS) * len(Gather.SLOTS)
    buf = {key: pltpu.VMEM((2, 4, 4, 4, ROWS[key[0]][key[1]], 128), BF16) for key in BUFS}
    passed = pl.pallas_call(
        early_kernel,
        out_shape=[buf[0, a] for a in range(3)] + [
            pltpu.VMEM((PAIRS - 1, WIDTH, D), BF16),
            pltpu.VMEM((LAYERS - 1, TOKENS, WIDTH), BF16),
            pltpu.VMEM((TOKENS, WIDTH), F32),
            pltpu.VMEM((LAYERS, WIDTH, TOKENS), BF16),
            pltpu.VMEM((LAYERS, TOKENS, WIDTH), BF16),
            pltpu.VMEM((1, WIDTH, D), BF16),
        ],
        in_specs=[hbm] * 4,
        out_specs=[vmem] * 9,
        scratch_shapes=[buf[g, a] for g, a in BUFS if g] + [
            pltpu.VMEM((LAYERS, TOKENS, WIDTH), BF16),
            pltpu.VMEM((LAYERS, 2, TOKENS), jnp.int32),
            pltpu.VMEM((PAIRS - 1, WIDTH, D), BF16),
            pltpu.VMEM((LAYERS - 2, TOKENS, WIDTH), F32),
            pltpu.SemaphoreType.DMA((len(BUFS),)),
            pltpu.SemaphoreType.DMA((sems,)),
            pltpu.SemaphoreType.DMA((sems,)),
            pltpu.SemaphoreType.DMA((6,)),
        ],
        compiler_params=pltpu.CompilerParams(collective_id=0, has_side_effects=True, vmem_limit_bytes=EARLY_LIMIT),
        name="gather_and_products",
    )(cotangent, activations, mask, decoder)
    return tuple(pl.pallas_call(
        late_kernel,
        out_shape=[jax.ShapeDtypeStruct((PAIRS, WIDTH, D), BF16), jax.ShapeDtypeStruct((LAYERS, TOKENS, WIDTH), BF16)],
        in_specs=[vmem] * 9,
        out_specs=[hbm, hbm],
        scratch_shapes=[
            pltpu.VMEM((1, WIDTH, D), BF16),
            pltpu.VMEM((TOKENS, WIDTH), BF16),
            pltpu.SemaphoreType.DMA((4,)),
        ],
        compiler_params=pltpu.CompilerParams(vmem_limit_bytes=LATE_LIMIT),
        name="last_products",
    )(*passed))


def solution(mesh):
    in_specs = (
        P(None, None, ("layer", "feat")),
        P(None, None, ("layer", "feat")),
        P(None, "layer", "feat"),
        P(None, ("layer", "feat"), None),
    )
    out_specs = (P(None, ("layer", "feat"), None), P(None, None, ("layer", "feat")))
    return jax.shard_map(body, mesh=mesh, in_specs=in_specs, out_specs=out_specs, check_vma=False)
```

time: 217 us -> 67.5 us (0.31)
  waiting for transfers between devices: 146 us -> 0 us
  Pallas kernels: 0 us -> 66.7 us
  matrix products: 39.1 us -> 0 us
  between operations: 14.2 us -> 0.64 us
  other arithmetic: 11 us -> 0 us
  local copies, waits for them, and re-layouts: 6.11 us -> 0 us
    all_gather x2 -> x0, waiting for transfers between devices: 146 us -> none  [the longest x1 94.6 us: body(): upstream = lax.all_gather(cot_rows, 'feat', axis=2, tiled=True)]
    pallas_call x0 -> x2, Pallas kernels: none -> 66.7 us  [the longest x1 61.3 us: body(): pl.pallas_call(early_kernel, out_shape=[buf[0, a] for a in range(3)] + [p...]
    dot_general x8 -> x0, matrix products: 39.1 us -> none  [the longest x4 21.9 us: pair_work(): jnp.einsum('td,sfd->stf', upstream[target], rows, preferred_element_type=...]
    concatenate x1 -> x0, other arithmetic: 8.37 us -> none  [pair_work(): return (jnp.concatenate(grads, axis=0), partial_value)]
    unnamed x18 -> x0, local copies, waits for them, and re-layouts: 5.6 us -> none
    convert_element_type x2 -> x0, other arithmetic: 2.67 us -> none  [the longest x1 1.9 us: body(): (activations.astype(jnp.float32) * feature_mask).astype(jnp.bfloat16)]
  transfers between devices with their start and end apart: 2 -> 0, of which waited for: 2 -> 0; matrix products, arithmetic and copies ran while one was open for 3% -> 0% of each run, Pallas kernels for 0% -> 0%
where the time goes in v2:
time: 67.5 us; the launch traced here: 67.4 us
  Pallas kernels  66.7 us (99%)
    pallas_call x1, Pallas kernels, body(): pl.pallas_call(early_kernel, out_shape=[buf[0, a] for a in range(3)] + [p...  61.3 us
    pallas_call x1, Pallas kernels, body(): pl.pallas_call(late_kernel, out_shape=[jax.ShapeDtypeStruct((PAIRS, WIDTH...  5.46 us

profile of v2, /device:TPU:1, one launch (start us, length us, event | category | flops | bytes accessed | tf_op | source)
XLA Modules:
  0.0 67.4 jit_solution(14615751056028015136)
XLA Ops:
  0.6 61.3 %gather_and_products.1 = (bf16[2,4,4,4,48,128]{5,4,3,2,1,0:T(8,128)(2,1)S(1)}, bf16[2,4,4,4,48,128]{5,4,3,2,1,0:T(8,128)(2,1)S(1)}, bf16[2,4,4,4,32,128]{5,4,3,2...) custom-call(bf16[4,128,128]{2,1,0:T(8,128)(2,1)} %own_ref.1, ...), custom_call_target="tpu_custom_call" | custom-call | tf_op jit(solution)/shard_map/gather_and_products/pallas_call | solution.py:346
  61.9 5.5 %last_products.1 = (bf16[10,256,2048]{2,1,0:T(8,128)(2,1)}, bf16[4,1024,256]{2,1,0:T(8,128)(2,1)}) custom-call(bf16[2,4,4,4,48,128]{5,4,3,2,1,0:T(8,128)(2,1)S(1)} %get-tuple-element.11.refs_0_, bf16[2,4,4,4,48,128]{5,4,3,2,1,0:T(8,128)(2,1)S(1)} %get-tuple-element.12.refs_1_, bf16[2,4,4,4,32,128]{5,4,3,2,1,0:T(8,128)(2,1)S(1)} %get-tuple-element.13.refs_2_, ...), custom_call_target="tpu_custom_call" | custom-call | tf_op jit(solution)/shard_map/last_products/pallas_call | solution.py:371

commit v3 on v2

--- a/solution.py
+++ b/solution.py
@@ -17,8 +17,16 @@
 OFFSET = (0, 1, 3, 6)
 BUFS = [(g, a) for g in range(LAYERS) for a in range(3)]
 BF16, F32 = jnp.bfloat16, jnp.float32
-DIRECT = (3,)
-EARLY_LIMIT, LATE_LIMIT = 32 * 2**20, 6 * 2**20
+DIRECT = (3, 2)
+PIECES = (2, 2, 2, 2)
+STEPS = (2, 2, 2, 4)
+SCHEDULE = (
+    "p1 3", "p1 2", "p1 0", "p1 1", "prep 0", "prep 1", "prep 2", "prep 3", "p2 3", "p2 0", "p2 2", "p2 1",
+    "p3 3", "p2f 1", "p2f 0", "p3f 3", "p3 2", "sides 3", "p3 1", "last 3", "p3f 2", "p3 0", "work 3 0",
+    "sides 2", "work 3 1", "work 3 2", "last 2", "p3f 1", "work 3 3", "p3f 0", "sides 1", "work 2 0", "last 1",
+    "sides 0", "work 2 1", "last 0", "work 1 0", "work 1 1",
+)
+EARLY_LIMIT, LATE_LIMIT = 36 * 2**20, 6 * 2**20
 
 
 def position():
@@ -37,9 +45,12 @@
     return tuple(lax.rem(v + by + 4, 4) if i == axis else v for i, v in enumerate(c))
 
 
+SLOTS = {g: ("1L", "1R", "1O", "2L", "2R", "2O", *(f"3{side}{i}" for side in "LRO" for i in range(PIECES[g])), "p0", "pL", "pR", "pO")
+         for g in range(LAYERS)}
+INDEX = {key: i for i, key in enumerate((g, a, slot) for g in SLOTS for a in range(3) for slot in SLOTS[g])}
+
+
 class Gather:
-    SLOTS = ("1L", "1R", "1O", "2L", "2R", "2O", "3L0", "3L1", "3R0", "3R1", "3O0", "3O1", "p0", "pL", "pR", "pO")
-
     def __init__(self, own_ref, bufs, own_sem, send, recv):
         self.c, self.core = position()
         self.own_ref, self.bufs = own_ref, bufs
@@ -80,7 +91,7 @@
             if phase == "1" or (phase == "2" and g in DIRECT):
                 to = self.near(axis, 2)
             else:
-                by = (-1 if slot[2] == "0" else 1) if phase == "3" else (-1 if (g + a) % 2 else 1)
+                by = (-1 if int(slot[2]) < PIECES[g] // 2 else 1) if phase == "3" else (-1 if (g + a) % 2 else 1)
                 to = self.near(axis, -by)
         else:
             to = self.near(axis, 1 if side == "L" else -1)
@@ -91,8 +102,9 @@
         elif phase == "2":
             buf = buf.at[c2]
         elif phase == "3":
-            buf = buf.at[pl.ds(2 * int(slot[2]), 2)]
-        i = (g * 3 + a) * len(self.SLOTS) + self.SLOTS.index(slot)
+            size = 4 // PIECES[g]
+            buf = buf.at[pl.ds(size * int(slot[2]), size)]
+        i = INDEX[g, a, slot]
         return pltpu.make_async_remote_copy(
             src_ref=buf, dst_ref=buf, send_sem=self.send.at[i], recv_sem=self.recv.at[i],
             device_id=to, device_id_type=MESH)
@@ -116,7 +128,7 @@
                 self.go(g, a, "2O")
             self.go(g, a, "2L", "2R")
 
-    def p2_forward(self, g):
+    def p2f(self, g):
         for a in range(3):
             self.wait(g, a, "2L", "2R")
             self.go(g, a, "2O")
@@ -126,27 +138,39 @@
             if g in DIRECT:
                 self.wait(g, a, "2L", "2R")
             self.wait(g, a, "2O")
-            self.go(g, a, "3L0", "3R1", "3L1", "3R0")
+            for i in range(PIECES[g]):
+                self.go(g, a, f"3L{i}", f"3R{PIECES[g] - 1 - i}")
         for a in range(3):
             self.go(g, a, "p0")
 
-    def p3_forward(self, g):
-        for a in range(3):
-            self.wait(g, a, "3L0")
-            self.go(g, a, "3O0")
-            self.wait(g, a, "3R1")
-            self.go(g, a, "3O1")
+    def p3_forward(self, g, i):
+        for a in range(3):
+            self.wait(g, a, f"3L{i}")
+            self.go(g, a, f"3O{i}")
+            j = PIECES[g] - 1 - i
+            self.wait(g, a, f"3R{j}")
+            self.go(g, a, f"3O{j}")
+
+    def p3f(self, g):
+        self.p3_forward(g, 0)
+
+    def p3g(self, g):
+        self.p3_forward(g, 1)
 
     def sides(self, g):
-        for a in range(3):
-            self.wait(g, a, "3L1")
+        half = PIECES[g] // 2
+        for a in range(3):
+            for i in range(half):
+                self.wait(g, a, f"3L{half + i}")
             self.go(g, a, "pL")
-            self.wait(g, a, "3R0")
+            for i in range(half):
+                self.wait(g, a, f"3R{i}")
             self.go(g, a, "pR")
 
     def last(self, g):
         for a in range(3):
-            self.wait(g, a, "3O0", "3O1")
+            for i in range(PIECES[g]):
+                self.wait(g, a, f"3O{i}")
             self.go(g, a, "pO")
 
     def arrived(self, g):
@@ -155,7 +179,7 @@
 
     def finish(self):
         for g, a in BUFS:
-            for slot in self.SLOTS:
+            for slot in SLOTS[g]:
                 self.copy(g, a, slot).wait_send()
 
 
@@ -195,17 +219,20 @@
             mask_cols[s, tok, b * 128:(b + 1) * 128] = m.T.astype(BF16)
 
 
-def grad_step(bufs, g, q, sparse_t, grad, base):
+def work(bufs, g, i, sparse_t, grad, dec, base, total, finish):
+    size, count = D // STEPS[g], TOKENS // STEPS[g]
     lhs = sparse_t[0:g + 1].reshape((g + 1) * WIDTH, TOKENS)
-    out = jnp.dot(lhs, columns(bufs, g, q), preferred_element_type=F32).astype(BF16)
-    grad[base:base + g + 1, :, pl.ds(pl.multiple_of(q * 256, 256), 256)] = out.reshape(g + 1, WIDTH, 256)
-
-
-def feature_step(bufs, g, h, dec, base, total, finish):
-    tok = pl.ds(pl.multiple_of(h * 256, 256), 256)
-    lhs = rows(bufs, g, h)
+    blocks = size // 256
+    rhs = jnp.concatenate([columns(bufs, g, i * blocks + k) for k in range(blocks)], axis=1)
+    out = jnp.dot(lhs, rhs, preferred_element_type=F32).astype(BF16)
+    grad[base:base + g + 1, :, pl.ds(pl.multiple_of(i * size, size), size)] = out.reshape(g + 1, WIDTH, size)
+    tok = pl.ds(pl.multiple_of(i * count, count), count)
+    blocks = count // 256
+    lhs = jnp.concatenate([rows(bufs, g, i * blocks + k) for k in range(blocks)], axis=0)
+    rhs = dec[base:base + g + 1].reshape((g + 1) * WIDTH, D)
+    terms = lax.dot_general(lhs, rhs, (((1,), (1,)), ((), ())), preferred_element_type=F32)
     for s in range(g + 1):
-        term = lax.dot_general(lhs, dec[base + s], (((1,), (1,)), ((), ())), preferred_element_type=F32)
+        term = terms[:, s * WIDTH:(s + 1) * WIDTH]
         if g < LAYERS - 1:
             term = term + total[s, tok]
         if s == g:
@@ -214,12 +241,30 @@
             total[s, tok] = term
 
 
-def at(table, i):
-    for when, events in table:
-        @pl.when(i == when)
-        def _():
-            for event in events:
-                event()
+def plan():
+    before, steps = {}, []
+    for entry in SCHEDULE:
+        name, *numbers = entry.split()
+        numbers = [int(v) for v in numbers]
+        if name in ("prep", "work"):
+            before[name, *numbers] = steps
+            steps = []
+        else:
+            steps.append((name, numbers[0]))
+    return before, steps
+
+
+def run(net, steps):
+    for name, g in steps:
+        getattr(net, name)(g)
+
+
+def at(net, before, g, i):
+    for k in range(1, STEPS[g]):
+        if before["work", g, k]:
+            @pl.when(i == k)
+            def _():
+                run(net, before["work", g, k])
 
 
 def early_kernel(own_ref, act_hbm, mask_hbm, dec_hbm, *rest):
@@ -238,58 +283,34 @@
     for copy in own:
         copy.wait()
     net.meet()
-    for g in TARGETS:
-        net.p1(g)
     loads = [pltpu.make_async_copy(dec_hbm.at[pl.ds(6, 4)], dec.at[pl.ds(5, 4)], sem.at[1]),
              pltpu.make_async_copy(dec_hbm.at[pl.ds(3, 3)], dec.at[pl.ds(2, 3)], sem.at[2]),
              pltpu.make_async_copy(dec_hbm.at[pl.ds(1, 2)], dec.at[pl.ds(0, 2)], sem.at[3]),
              pltpu.make_async_copy(dec_hbm.at[pl.ds(0, 1)], dec0, sem.at[4])]
-    for load in loads:
-        load.start()
-    load_act.wait()
-    load_mask.wait()
-    prepare(0, act, mask, sparse_t, mask_cols)
-    prepare(1, act, mask, sparse_t, mask_cols)
-    net.p2(3)
-    net.p2(2)
-    prepare(2, act, mask, sparse_t, mask_cols)
-    prepare(3, act, mask, sparse_t, mask_cols)
-    net.p3(3)
-    net.p2(1)
-    net.p2_forward(2)
-    net.p3_forward(3)
-    net.p2_forward(1)
-    net.sides(3)
-    net.p3(2)
-    net.p2(0)
-    net.last(3)
-    net.arrived(3)
 
     def finish(s, tok, term):
         feat[s - 1, tok] = (term * mask_cols[s, tok].astype(F32)).astype(BF16)
 
-    plan = {
-        3: ([(1, [lambda: net.p3_forward(2)]), (2, [lambda: net.p2_forward(0), lambda: net.p3(1)]), (5, [lambda: net.sides(2)])],
-            [(0, [lambda: net.last(2)]), (3, [lambda: net.p3_forward(1), lambda: net.p3(0)])]),
-        2: ([(2, [lambda: net.sides(1)]), (6, [lambda: net.last(1)])],
-            [(1, [lambda: net.p3_forward(0)])]),
-        1: ([(1, [lambda: net.sides(0)]), (6, [lambda: net.last(0)])], []),
-    }
+    before, tail = plan()
+    for s in range(LAYERS):
+        run(net, before["prep", s])
+        if s == 0:
+            for load in loads:
+                load.start()
+            load_act.wait()
+            load_mask.wait()
+        prepare(s, act, mask, sparse_t, mask_cols)
     for i, g in enumerate((3, 2, 1)):
         base = OFFSET[g] - 1
-        if g < 3:
-            net.arrived(g)
+        run(net, before["work", g, 0])
+        net.arrived(g)
         loads[i].wait()
 
-        @pl.loop(0, 8)
-        def _(q):
-            at(plan[g][0], q)
-            grad_step(bufs, g, q, sparse_t, grad, base)
-
-        @pl.loop(0, 4)
-        def _(h):
-            at(plan[g][1], h)
-            feature_step(bufs, g, h, dec, base, TOTAL(total, total0), finish)
+        @pl.loop(0, STEPS[g])
+        def _(k):
+            at(net, before, g, k)
+            work(bufs, g, k, sparse_t, grad, dec, base, TOTAL(total, total0), finish)
+    run(net, tail)
     loads[3].wait()
     net.arrived(0)
     net.finish()
@@ -322,17 +343,13 @@
     def finish(s, tok, term):
         feat[tok] = (term * mask_cols[0, tok].astype(F32)).astype(BF16)
 
-    @pl.loop(0, 4)
-    def _(h):
-        feature_step(bufs, 0, h, dec0.at[pl.ds(0, 1)], 0, TOTAL(None, total0), finish)
-    stores.append(pltpu.make_async_copy(feat, feat_hbm.at[0], sem.at[2]))
-    stores[-1].start()
-
-    @pl.loop(0, 8)
-    def _(q):
-        grad_step(bufs, 0, q, sparse_t, grad, 0)
-    stores.append(pltpu.make_async_copy(grad, grad_hbm.at[pl.ds(0, 1)], sem.at[3]))
-    stores[-1].start()
+    @pl.loop(0, STEPS[0])
+    def _(k):
+        work(bufs, 0, k, sparse_t, grad, dec0, 0, TOTAL(None, total0), finish)
+    stores += [pltpu.make_async_copy(feat, feat_hbm.at[0], sem.at[2]),
+               pltpu.make_async_copy(grad, grad_hbm.at[pl.ds(0, 1)], sem.at[3])]
+    for out in stores[2:]:
+        out.start()
     for out in stores:
         out.wait()
 
@@ -341,7 +358,7 @@
     vmem, hbm = pl.BlockSpec(memory_space=pltpu.VMEM), pl.BlockSpec(memory_space=pltpu.HBM)
     mask = pltpu.with_memory_space_constraint(jnp.transpose(active_blocks, (0, 2, 1)), pltpu.HBM)
     cotangent = pltpu.with_memory_space_constraint(cotangent, pltpu.HBM)
-    sems = len(BUFS) * len(Gather.SLOTS)
+    sems = len(INDEX)
     buf = {key: pltpu.VMEM((2, 4, 4, 4, ROWS[key[0]][key[1]], 128), BF16) for key in BUFS}
     passed = pl.pallas_call(
         early_kernel,

time: 67.5 us -> 59.7 us (0.88)
  Pallas kernels: 66.7 us -> 58.9 us
    pallas_call x1, Pallas kernels: 61.3 us -> 54.2 us  [body(): pl.pallas_call(early_kernel, out_shape=[buf[0, a] for a in range(3)] + [p...]
    pallas_call x1, Pallas kernels: 5.46 us -> 4.75 us  [body(): pl.pallas_call(late_kernel, out_shape=[jax.ShapeDtypeStruct((PAIRS, WIDTH...]
where the time goes in v3:
time: 59.7 us; the launch traced here: 59.6 us
  Pallas kernels  58.9 us (99%)
  between operations  0.64 us (1%)
    pallas_call x1, Pallas kernels, body(): pl.pallas_call(early_kernel, out_shape=[buf[0, a] for a in range(3)] + [p...  54.2 us
    pallas_call x1, Pallas kernels, body(): pl.pallas_call(late_kernel, out_shape=[jax.ShapeDtypeStruct((PAIRS, WIDTH...  4.75 us

profile of v3, /device:TPU:1, one launch (start us, length us, event | category | flops | bytes accessed | tf_op | source)
XLA Modules:
  0.0 59.6 jit_solution(3654711530099328270)
XLA Ops:
  0.6 54.2 %gather_and_products.1 = (bf16[2,4,4,4,48,128]{5,4,3,2,1,0:T(8,128)(2,1)S(1)}, bf16[2,4,4,4,48,128]{5,4,3,2,1,0:T(8,128)(2,1)S(1)}, bf16[2,4,4,4,32,128]{5,4,3,2...) custom-call(bf16[4,128,128]{2,1,0:T(8,128)(2,1)} %own_ref.1, ...), custom_call_target="tpu_custom_call" | custom-call | tf_op jit(solution)/shard_map/gather_and_products/pallas_call | solution.py:363
  54.8 4.7 %last_products.1 = (bf16[10,256,2048]{2,1,0:T(8,128)(2,1)}, bf16[4,1024,256]{2,1,0:T(8,128)(2,1)}) custom-call(bf16[2,4,4,4,48,128]{5,4,3,2,1,0:T(8,128)(2,1)S(1)} %get-tuple-element.11.refs_0_, bf16[2,4,4,4,48,128]{5,4,3,2,1,0:T(8,128)(2,1)S(1)} %get-tuple-element.12.refs_1_, bf16[2,4,4,4,32,128]{5,4,3,2,1,0:T(8,128)(2,1)S(1)} %get-tuple-element.13.refs_2_, ...), custom_call_target="tpu_custom_call" | custom-call | tf_op jit(solution)/shard_map/last_products/pallas_call | solution.py:388

commit v4 on v3

--- a/solution.py
+++ b/solution.py
@@ -20,11 +20,12 @@
 DIRECT = (3, 2)
 PIECES = (2, 2, 2, 2)
 STEPS = (2, 2, 2, 4)
+SPLIT, OWN_STEPS = (3,), 1
 SCHEDULE = (
     "p1 3", "p1 2", "p1 0", "p1 1", "prep 0", "prep 1", "prep 2", "prep 3", "p2 3", "p2 0", "p2 2", "p2 1",
-    "p3 3", "p2f 1", "p2f 0", "p3f 3", "p3 2", "sides 3", "p3 1", "last 3", "p3f 2", "p3 0", "work 3 0",
-    "sides 2", "work 3 1", "work 3 2", "last 2", "p3f 1", "work 3 3", "p3f 0", "sides 1", "work 2 0", "last 1",
-    "sides 0", "work 2 1", "last 0", "work 1 0", "work 1 1",
+    "p3 3", "p2f 1", "p2f 0", "p3f 3", "p3 2", "p3 1", "sides 3", "last 3", "own 3 0", "p3f 2", "p3 0",
+    "work 3 0", "sides 2", "work 3 1", "work 3 2", "last 2", "p3f 1", "work 3 3", "p3f 0", "sides 1", "work 2 0",
+    "last 1", "sides 0", "work 2 1", "last 0", "work 1 0", "work 1 1",
 )
 EARLY_LIMIT, LATE_LIMIT = 36 * 2**20, 6 * 2**20
 
@@ -219,13 +220,35 @@
             mask_cols[s, tok, b * 128:(b + 1) * 128] = m.T.astype(BF16)
 
 
+def panel_products(bufs, g, panels, sparse_t, grad, base):
+    lhs = sparse_t[0:g + 1].reshape((g + 1) * WIDTH, TOKENS)
+    rhs = jnp.concatenate(
+        [jnp.concatenate([block(bufs, g, l % 4, y, (l // 4) * 2 + zl, core) for l in range(8)], axis=0)
+         for zl, y, core in panels], axis=1)
+    out = jnp.dot(lhs, rhs, preferred_element_type=F32).astype(BF16)
+    for k, (zl, y, core) in enumerate(panels):
+        at = pl.ds(pl.multiple_of(((zl * 4 + y) * 2 + core) * 128, 128), 128)
+        grad[base:base + g + 1, :, at] = out[:, k * 128:(k + 1) * 128].reshape(g + 1, WIDTH, 128)
+
+
+def own_work(bufs, g, i, sparse_t, grad, base):
+    core = position()[1]
+    panels = [(i, y, core) for y in range(4)] if OWN_STEPS == 2 else [(zl, y, core) for zl in range(2) for y in range(4)]
+    panel_products(bufs, g, panels, sparse_t, grad, base)
+
+
 def work(bufs, g, i, sparse_t, grad, dec, base, total, finish):
     size, count = D // STEPS[g], TOKENS // STEPS[g]
-    lhs = sparse_t[0:g + 1].reshape((g + 1) * WIDTH, TOKENS)
     blocks = size // 256
-    rhs = jnp.concatenate([columns(bufs, g, i * blocks + k) for k in range(blocks)], axis=1)
-    out = jnp.dot(lhs, rhs, preferred_element_type=F32).astype(BF16)
-    grad[base:base + g + 1, :, pl.ds(pl.multiple_of(i * size, size), size)] = out.reshape(g + 1, WIDTH, size)
+    if g in SPLIT:
+        other = 1 - position()[1]
+        panels = [((i * blocks + k) // 4, lax.rem(i * blocks + k, 4), other) for k in range(blocks)]
+        panel_products(bufs, g, panels, sparse_t, grad, base)
+    else:
+        lhs = sparse_t[0:g + 1].reshape((g + 1) * WIDTH, TOKENS)
+        rhs = jnp.concatenate([columns(bufs, g, i * blocks + k) for k in range(blocks)], axis=1)
+        out = jnp.dot(lhs, rhs, preferred_element_type=F32).astype(BF16)
+        grad[base:base + g + 1, :, pl.ds(pl.multiple_of(i * size, size), size)] = out.reshape(g + 1, WIDTH, size)
     tok = pl.ds(pl.multiple_of(i * count, count), count)
     blocks = count // 256
     lhs = jnp.concatenate([rows(bufs, g, i * blocks + k) for k in range(blocks)], axis=0)
@@ -246,7 +269,7 @@
     for entry in SCHEDULE:
         name, *numbers = entry.split()
         numbers = [int(v) for v in numbers]
-        if name in ("prep", "work"):
+        if name in ("prep", "work", "own"):
             before[name, *numbers] = steps
             steps = []
         else:
@@ -289,7 +312,7 @@
              pltpu.make_async_copy(dec_hbm.at[pl.ds(0, 1)], dec0, sem.at[4])]
 
     def finish(s, tok, term):
-        feat[s - 1, tok] = (term * mask_cols[s, tok].astype(F32)).astype(BF16)
+        feat[s - 1, tok] = term.astype(BF16) * mask_cols[s, tok]
 
     before, tail = plan()
     for s in range(LAYERS):
@@ -302,6 +325,14 @@
         prepare(s, act, mask, sparse_t, mask_cols)
     for i, g in enumerate((3, 2, 1)):
         base = OFFSET[g] - 1
+        if g in SPLIT:
+            run(net, before["own", g, 0])
+
+            @pl.loop(0, OWN_STEPS)
+            def _(k):
+                if OWN_STEPS > 1 and before["own", g, 1]:
+                    pl.when(k == 1)(lambda: run(net, before["own", g, 1]))
+                own_work(bufs, g, k, sparse_t, grad, base)
         run(net, before["work", g, 0])
         net.arrived(g)
         loads[i].wait()
@@ -341,7 +372,7 @@
         out.start()
 
     def finish(s, tok, term):
-        feat[tok] = (term * mask_cols[0, tok].astype(F32)).astype(BF16)
+        feat[tok] = term.astype(BF16) * mask_cols[0, tok]
 
     @pl.loop(0, STEPS[0])
     def _(k):

time: 59.7 us -> 59 us (0.988)
  Pallas kernels: 58.9 us -> 58.2 us
    pallas_call x1, Pallas kernels: 54.2 us -> 53.4 us  [body(): pl.pallas_call(early_kernel, out_shape=[buf[0, a] for a in range(3)] + [p...]
where the time goes in v4:
time: 59 us; the launch traced here: 58.8 us
  Pallas kernels  58.2 us (99%)
  between operations  0.64 us (1%)
    pallas_call x1, Pallas kernels, body(): pl.pallas_call(early_kernel, out_shape=[buf[0, a] for a in range(3)] + [p...  53.4 us
    pallas_call x1, Pallas kernels, body(): pl.pallas_call(late_kernel, out_shape=[jax.ShapeDtypeStruct((PAIRS, WIDTH...  4.75 us

profile of v4, /device:TPU:1, one launch (start us, length us, event | category | flops | bytes accessed | tf_op | source)
XLA Modules:
  0.0 58.8 jit_solution(15617976805567316102)
XLA Ops:
  0.6 53.4 %gather_and_products.1 = (bf16[2,4,4,4,48,128]{5,4,3,2,1,0:T(8,128)(2,1)S(1)}, bf16[2,4,4,4,48,128]{5,4,3,2,1,0:T(8,128)(2,1)S(1)}, bf16[2,4,4,4,32,128]{5,4,3,2...) custom-call(bf16[4,128,128]{2,1,0:T(8,128)(2,1)} %own_ref.1, ...), custom_call_target="tpu_custom_call" | custom-call | tf_op jit(solution)/shard_map/gather_and_products/pallas_call | solution.py:394
  54.1 4.7 %last_products.1 = (bf16[10,256,2048]{2,1,0:T(8,128)(2,1)}, bf16[4,1024,256]{2,1,0:T(8,128)(2,1)}) custom-call(bf16[2,4,4,4,48,128]{5,4,3,2,1,0:T(8,128)(2,1)S(1)} %get-tuple-element.11.refs_0_, bf16[2,4,4,4,48,128]{5,4,3,2,1,0:T(8,128)(2,1)S(1)} %get-tuple-element.12.refs_1_, bf16[2,4,4,4,32,128]{5,4,3,2,1,0:T(8,128)(2,1)S(1)} %get-tuple-element.13.refs_2_, ...), custom_call_target="tpu_custom_call" | custom-call | tf_op jit(solution)/shard_map/last_products/pallas_call | solution.py:419
